TPU v7x, 128 devices: a whole 4x4x4 slice. The times are simulated.
128 devices in a mesh: dp: 64 (over x, z, y), rep: 2 (over core).
Axes of the slice: x: 4, y: 4, z: 4, core: 2. Of those that a mesh axis runs over, the one named last changes fastest.
Arguments:
- pooled: bfloat16 [16, 128, 32768], P(None, ('dp', 'rep')), may hold values from -6 to 6
- slot_of_block: int32 [128], replicated, may hold values from 0 to 127, each once
- dense_part: bfloat16 [128, 32768], P(None, ('dp', 'rep')), may hold values from -6 to 6
- labels: int32 [32768], P(('dp', 'rep')), may hold values 0 or 1
- sample_weight: float32 [32768], P(('dp', 'rep')), may hold values from 0.5 to 18, as said below
- proj_wide: bfloat16 [6, 256, 128], replicated, may hold values from -0.375 to 0.375
- proj_mid: bfloat16 [4, 64, 128], replicated, may hold values from -0.75 to 0.75
- proj_narrow: bfloat16 [16, 16, 128], replicated, may hold values from -1.5 to 1.5
- cross_in: bfloat16 [2, 3456, 256], replicated, may hold values from -0.109375 to 0.109375
- cross_out: bfloat16 [2, 256, 3456], replicated, may hold values from -0.375 to 0.375
- cross_bias: float32 [2, 3456], replicated, may hold values from -3 to 3
- head_weight: float32 [3456], replicated, may hold values from -0.24 to 0.24
Outputs:
- pooled_grad: float32 [16, 128, 32768], P(None, ('dp', 'rep'))
- grad_cross_in: float32 [2, 3456, 256], P(None, ('dp', 'rep'))
- grad_cross_out: float32 [2, 256, 3456], P(None, None, ('dp', 'rep'))
- grad_bias: float32 [2, 3456], P(None, ('dp', 'rep'))
Inputs may be any that keep to these rules, and one draw needn't show every extreme that they name: `slot_of_block`: each number of 0 to 127 appears once. `sample_weight`: positive.
All inputs are finite; a program needn't handle non-finite values. No bound on the sum of `labels` on one device may be relied on, other than what follows from the above.
Results may differ from a plain program's by a relative error of at most 0.014.
Values may be sent and summed in bfloat16 or wider, within the bound.
A program may use at most 128 MiB of HBM per device.

v0:
```python
import jax
import jax.numpy as jnp
from jax import lax
from jax.sharding import Mesh
from jax.sharding import PartitionSpec as P

BLOCK_WIDTH = 16
WIDE_TABLES = 6
MID_TABLES = 4
NARROW_TABLES = 16
WIDE_WIDTH = 256
MID_WIDTH = 64
NARROW_WIDTH = 16
PROJECTED = 128
LAYERS = 2
BLOCKS = 128
DP = ("dp_0", "dp_1", "dp_2")
DP_REP = ("dp_0", "dp_1", "dp_2", "rep")


def split_up(shard, dim, devices):
    before, after = (shard.shape[:dim], shard.shape[dim + 1 :])
    return jnp.moveaxis(shard.reshape(*before, devices, -1, *after), dim, 0)


def joined_along(tiles, dim):
    dims = list(tiles.shape[1:])
    dims[dim] *= tiles.shape[0]
    return jnp.moveaxis(tiles, 0, dim).reshape(dims)


def one_exchange(shard, axis, axes, splits, concats):
    sizes = [lax.axis_size(a) for a in axes]
    tiles = split_up(shard, splits[0], sizes[0])
    tiles = jnp.moveaxis(split_up(tiles, splits[1] + 1, sizes[1]), 0, 1)
    inside = tiles.shape[2:]
    tiles = tiles.reshape(-1, *inside)
    tiles = lax.all_to_all(tiles, axis, split_axis=0, concat_axis=0, tiled=True)
    tiles = joined_along(tiles.reshape(*sizes, *inside), concats[0] + 1)
    return joined_along(tiles, concats[1])


def one_axis_at_a_time(shard, axes):
    for axis in axes:
        shard = lax.psum(shard, axis)
    return shard


def own_tiles(shard, axis, dim):
    devices = lax.axis_size(axis)
    tiles = split_up(shard, dim, devices)
    lines = tiles.reshape(devices, -1)
    extent = max(16, -(-lines.shape[1] // 1024) * 8)
    lines = jnp.pad(lines, ((0, 0), (0, extent * 128 - lines.shape[1]))).reshape(-1, 128)
    own = lax.psum_scatter(lines, axis, scatter_dimension=0, tiled=True)
    return own.reshape(-1)[: tiles[0].size].reshape(tiles.shape[1:])


def table_layout():
    first_end = WIDE_TABLES * (WIDE_WIDTH // BLOCK_WIDTH)
    second_end = first_end + MID_TABLES * (MID_WIDTH // BLOCK_WIDTH)
    return (
        (0, first_end, WIDE_TABLES, WIDE_WIDTH),
        (first_end, second_end, MID_TABLES, MID_WIDTH),
        (second_end, BLOCKS, NARROW_TABLES, NARROW_WIDTH),
    )


def project_tables(logical, proj_tables):
    row_count = logical.shape[2]
    outputs = []
    for layout, proj_table in zip(table_layout(), proj_tables):
        block_start, block_end, table_count, table_width = layout
        pieces = logical[:, block_start:block_end].reshape(
            BLOCK_WIDTH, table_count, table_width // BLOCK_WIDTH, row_count
        )
        matrix = proj_table.reshape(table_count, table_width // BLOCK_WIDTH, BLOCK_WIDTH, PROJECTED)
        result = jnp.einsum("tkco,ctkr->tor", matrix, pieces, preferred_element_type=jnp.float32)
        outputs.append(result.reshape(table_count * PROJECTED, row_count))
    return jnp.concatenate(outputs, 0)


def project_back(proj_grad, proj_tables):
    row_count = proj_grad.shape[1]
    outputs = []
    offset = 0
    for layout, proj_table in zip(table_layout(), proj_tables):
        block_start, block_end, table_count, table_width = layout
        piece = proj_grad[offset : offset + table_count * PROJECTED].reshape(
            table_count, PROJECTED, row_count
        )
        offset = offset + table_count * PROJECTED
        matrix = proj_table.reshape(table_count, table_width // BLOCK_WIDTH, BLOCK_WIDTH, PROJECTED)
        result = jnp.einsum("tkco,tor->ctkr", matrix, piece, preferred_element_type=jnp.float32)
        outputs.append(result.reshape(BLOCK_WIDTH, block_end - block_start, row_count))
    return jnp.concatenate(outputs, 1)


def block_step(
    slots,
    dense_part,
    labels,
    sample_weight,
    slot_of_block,
    proj_tables,
    cross_in,
    cross_out,
    cross_bias,
    head_weight,
):
    logical = jnp.take(slots, slot_of_block, axis=1)
    projected = project_tables(logical, proj_tables)
    start = jnp.concatenate([dense_part.astype(jnp.float32), projected], 0).astype(jnp.bfloat16)
    start_full = start.astype(jnp.float32)
    layer_inputs = [start]
    hidden_list = []
    gate_list = []
    current = start
    for layer in range(LAYERS):
        hidden = jnp.einsum(
            "wk,wr->kr", cross_in[layer], current, preferred_element_type=jnp.float32
        ).astype(jnp.bfloat16)
        gate = (
            jnp.einsum("kw,kr->wr", cross_out[layer], hidden, preferred_element_type=jnp.float32)
            + cross_bias[layer][:, None]
        )
        current = (start_full * gate + current.astype(jnp.float32)).astype(jnp.bfloat16)
        hidden_list.append(hidden)
        gate_list.append(gate)
        layer_inputs.append(current)
    logit = jnp.dot(head_weight, current.astype(jnp.float32), precision=lax.Precision.HIGHEST)
    signal = sample_weight * (jax.nn.sigmoid(logit) - labels.astype(jnp.float32))
    upstream = head_weight[:, None] * signal[None, :]
    start_grad = jnp.zeros(start_full.shape, jnp.float32)
    in_terms = [None] * LAYERS
    out_terms = [None] * LAYERS
    bias_terms = [None] * LAYERS
    for layer in reversed(range(LAYERS)):
        gate_grad = start_full * upstream
        bias_terms[layer] = jnp.sum(gate_grad, axis=1)
        gate_low = gate_grad.astype(jnp.bfloat16)
        out_terms[layer] = jnp.einsum(
            "wr,kr->wk", gate_low, hidden_list[layer], preferred_element_type=jnp.float32
        )
        hidden_grad = jnp.einsum(
            "kw,wr->kr", cross_out[layer], gate_low, preferred_element_type=jnp.float32
        ).astype(jnp.bfloat16)
        in_terms[layer] = jnp.einsum(
            "wr,kr->wk", layer_inputs[layer], hidden_grad, preferred_element_type=jnp.float32
        )
        start_grad = start_grad + gate_list[layer] * upstream
        upstream = upstream + jnp.einsum(
            "wk,kr->wr", cross_in[layer], hidden_grad, preferred_element_type=jnp.float32
        )
    start_grad = start_grad + upstream
    proj_grad = start_grad[PROJECTED:].astype(jnp.bfloat16)
    logical_grad = project_back(proj_grad, proj_tables)
    slot_grad = jnp.zeros(logical_grad.shape, jnp.float32).at[:, slot_of_block, :].set(logical_grad)
    return (slot_grad, jnp.stack(in_terms), jnp.stack(out_terms), jnp.stack(bias_terms))


def body(
    pooled,
    slot_of_block,
    dense_part,
    labels,
    sample_weight,
    proj_wide,
    proj_mid,
    proj_narrow,
    cross_in,
    cross_out,
    cross_bias,
    head_weight,
):
    dp_count = lax.axis_size(DP)
    rep_count = lax.axis_size("rep")
    devices = dp_count * rep_count
    row_count = labels.shape[0]
    blocks_here = pooled.shape[1]
    batch_rows = row_count * devices
    layer_count = cross_in.shape[0]
    received = one_exchange(pooled[:, None, None], DP_REP, (DP, "rep"), (4, 4), (1, 2))
    slots = received.reshape(BLOCK_WIDTH, BLOCKS, row_count)
    local_total = jnp.sum(sample_weight)
    total = one_axis_at_a_time(local_total, DP_REP)
    proj_tables = (proj_wide, proj_mid, proj_narrow)
    slot_grad, in_term, out_term, bias_term = block_step(
        slots,
        dense_part,
        labels,
        sample_weight,
        slot_of_block,
        proj_tables,
        cross_in,
        cross_out,
        cross_bias,
        head_weight,
    )
    sectioned_grad = slot_grad.reshape(
        BLOCK_WIDTH, dp_count, rep_count, blocks_here, 1, 1, row_count
    )
    returned = lax.all_to_all(
        lax.all_to_all(
            sectioned_grad.astype(jnp.bfloat16), DP, split_axis=1, concat_axis=4, tiled=True
        ),
        "rep",
        split_axis=2,
        concat_axis=5,
        tiled=True,
    ).astype(sectioned_grad.dtype)
    returned = returned.reshape(BLOCK_WIDTH, blocks_here, batch_rows)
    weight_terms = jnp.concatenate([in_term, out_term], 0)
    weight_sums = own_tiles(weight_terms.astype(jnp.bfloat16), DP_REP, 1).astype(jnp.float32)
    bias_sums = lax.psum_scatter(bias_term, DP_REP, scatter_dimension=1, tiled=True)
    scale = batch_rows / total
    grad_in = weight_sums[:layer_count] * scale
    grad_out = jnp.swapaxes(weight_sums[layer_count:], 1, 2) * scale
    grad_bias = bias_sums * scale
    return (returned * scale, grad_in, grad_out, grad_bias)


def solution(mesh):
    finer = Mesh(mesh.devices.reshape(4, 4, 4, mesh.shape["rep"]), ("dp_0", "dp_1", "dp_2", "rep"))
    return jax.shard_map(
        body,
        mesh=finer,
        in_specs=(
            P(None, DP_REP, None),
            P(),
            P(None, DP_REP),
            P(DP_REP),
            P(DP_REP),
            P(),
            P(),
            P(),
            P(),
            P(),
            P(),
            P(),
        ),
        out_specs=(
            P(None, DP_REP, None),
            P(None, DP_REP, None),
            P(None, None, DP_REP),
            P(None, DP_REP),
        ),
        check_vma=False,
    )
```

profile of v0, /device:TPU:0, one launch (start us, length us, event | category | flops | bytes accessed | tf_op | source)
XLA Modules:
  0.0 294.4 jit_solution(1450464642006116457)
XLA Ops:
  7.2 1.6 copy.94
  9.1 1.6 copy.69
  10.6 11.2 %all-to-all-start = ((bf16[128,16,1,1,1,256]{5,1,4,3,2,0:T(8,128)(2,1)}), bf16[128,16,1,1,1,256]{5,1,4,3,2,0:T(8,128)(2,1)S(1)}, u32[]{:S(2)}, u32[]{:S(2)}) async-start(bf16[128,16,1,1,1,256]{5,1,4,3,2,0:T(8,128)(2,1)} %bitcast.2), calls=%async_computation | async-start | bytes 2097152 | tf_op jit(solution)/shard_map/all_to_all | solution.py:38
  21.9 0.7 copy.73
  22.6 0.6 reshape.183
  23.2 0.7 slice_reduce_fusion
  23.9 17.0 %all-to-all-done = bf16[128,16,1,1,1,256]{5,1,4,3,2,0:T(8,128)(2,1)S(1)} async-done(((bf16[128,16,1,1,1,256]{5,1,4,3,2,0:T(8,128)(2,1)}), bf16[128,16,1,1,1,256]{5,1,4,3,2,0:T(8,128)(2,1)S(1)}, u32[]{:S(2)}, u32[]{:S(2)}) %all-to-all-start) | async-done | bytes 1048608 | tf_op jit(solution)/shard_map/all_to_all | solution.py:38
  40.9 0.6 gather_fusion
  42.4 0.8 copy.76
  44.5 2.3 fusion.37
  47.2 2.5 fusion.8
  49.9 0.6 fusion.43
  50.6 0.7 fusion.1
  51.4 1.7 fusion.13
  53.8 0.7 fusion.46
  54.5 2.1 convolution_convert_fusion
  56.6 1.8 fusion.11
  58.4 0.8 fusion.40
  59.2 1.0 copy-done.3
  60.2 2.0 convolution_convert_fusion.1
  62.2 0.7 convolution_convert_fusion.2
  62.9 3.8 %concatenate.29 = bf16[1,128,27,256]{3,2,1,0:T(8,128)(2,1)} reshape(bf16[3456,256]{1,0:T(8,128)(2,1)} %convolution_convert_fusion) | data formatting | bytes 3538944 | tf_op jit(solution)/shard_map/concatenate | solution.py:213
  66.7 3.8 %concatenate.28 = bf16[1,128,27,256]{3,2,1,0:T(8,128)(2,1)} reshape(bf16[3456,256]{1,0:T(8,128)(2,1)} %convolution_convert_fusion.1) | data formatting | bytes 3538944 | tf_op jit(solution)/shard_map/concatenate | solution.py:213
  70.5 1.6 concatenate.27
  72.1 3.0 %convolution_convert_fusion.3 = bf16[3456,256]{1,0:T(8,128)(2,1)} fusion(bf16[256,256]{1,0:T(8,128)(2,1)S(1)} %fusion.40, bf16[2048,256]{0,1:T(8,128)(2,1)S(1)} %copy.76, bf16[512,256]{0,1:T(8,128)(2,1)} %copy-done.8, bf16[768,256]{0,1:T(8,128)(2,1)} %copy-done.6, bf16[128,256]{0,1:T(8,128)(2,1)S(1)} %copy-done.12), kind=kOutput, calls=%fused_computation.22 | convolution fusion | flops 460947456 | bytes 3670016 | tf_op jit(solution)/shard_map/wr,kr->wk/dot_general | solution.py:148
  75.1 3.9 %concatenate.26 = bf16[1,128,27,256]{3,2,1,0:T(8,128)(2,1)} reshape(bf16[3456,256]{1,0:T(8,128)(2,1)} %convolution_convert_fusion.3) | data formatting | bytes 3538944 | tf_op jit(solution)/shard_map/concatenate | solution.py:213
  79.0 6.7 %maximum_bitcast_fusion = bf16[128,4,27,256]{3,2,0,1:T(8,128)(2,1)} fusion(bf16[1,128,27,256]{3,2,1,0:T(8,128)(2,1)S(1)} %copy-done.2, bf16[1,128,27,256]{3,2,1,0:T(8,128)(2,1)} %concatenate.28, bf16[1,128,27,256]{3,2,1,0:T(8,128)(2,1)} %concatenate.27, bf16[1,128,27,256]{3,2,1,0:T(8,128)(2,1)} %concatenate.26), kind=kLoop, calls=%fused_computation.2 | loop fusion | flops 10616832 | bytes 14155776 | tf_op jit(solution)/shard_map/transpose | solution.py:23
  85.7 8.0 %copy.83 = bf16[128,4,27,256]{3,2,1,0:T(8,128)(2,1)} copy(bf16[128,4,27,256]{3,2,0,1:T(8,128)(2,1)} %maximum_bitcast_fusion) | data formatting | bytes 14155776 | tf_op jit(solution)/shard_map/transpose | solution.py:23
  93.8 12.5 %reshape.162 = bf16[27648,128]{1,0:T(8,128)(2,1)} reshape(bf16[128,4,27,256]{3,2,1,0:T(8,128)(2,1)} %copy.83) | data formatting | bytes 14155776 | tf_op jit(solution)/shard_map/reshape | solution.py:54
  106.3 0.7 copy-done.21
  107.0 5.7 %fusion.4 = bf16[3456,256]{0,1:T(8,128)(2,1)S(1)} fusion(f32[3456,256]{0,1:T(8,128)} %copy-done.3, bf16[256,256]{1,0:T(8,128)(2,1)S(1)} %fusion.40, f32[3456,256]{0,1:T(8,128)} %copy-done.1, f32[3456,256]{0,1:T(8,128)} %get-tuple-element.31, f32[256]{0:T(256)S(1)} %copy-done.21, f32[3456]{0:T(1024)S(1)} %copy-done.14, bf16[2,3456,256]{2,1,0:T(8,128)(2,1)} %param.20), kind=kOutput, calls=%fused_computation.18 | convolution fusion | flops 459177984 | bytes 14301696 | tf_op jit(solution)/shard_map/wk,kr->wr/dot_general | solution.py:152
  114.5 1.5 maximum_bitcast_fusion.1
  116.2 11.9 %scatter_fusion = f32[16,128,256]{2,0,1:T(8,128)S(1)} fusion(f32[16,128,256]{2,0,1:T(8,128)S(1)} %broadcast_in_dim.18, s32[128]{0:T(128)S(1)} %copy-done.23, f32[128,16,256]{2,1,0:T(8,128)} %maximum_bitcast_fusion.1), kind=kCustom, calls=%fused_computation.1 | custom fusion | bytes 6291968 | tf_op jit(solution)/shard_map/scatter | solution.py:158
  128.1 1.1 convert_element_type.89
  129.2 4.9 %all-to-all-start.1 = ((bf16[16,64,2,1,1,1,256]{6,0,2,5,4,3,1:T(8,128)(2,1)}), bf16[16,64,2,1,1,1,256]{6,0,2,5,4,3,1:T(8,128)(2,1)S(1)}, u32[]{:S(2)}, u32[]{:S(2)}) async-start(bf16[16,64,2,1,1,1,256]{6,0,2,5,4,3,1:T(8,128)(2,1)} %bitcast.47), calls=%async_computation.1 | async-start | bytes 2097152 | tf_op jit(solution)/shard_map/all_to_all | solution.py:204
  134.1 16.6 %psum.28 = f32[]{:T(128)} all-reduce(f32[]{:T(128)} %get-tuple-element.28), channel_id=1, replica_groups=mesh['dp_0'=4,'dp_1'=4,'dp_2'=4,'rep'=2] {'dp_0'}, use_global_device_ids=true, to_apply=%region_2.0 | all-reduce | flops 1 | bytes 8 | tf_op jit(solution)/shard_map/psum | solution.py:45
  150.7 11.1 %psum.29 = f32[]{:T(128)} all-reduce(f32[]{:T(128)} %psum.28), channel_id=1, replica_groups=mesh['dp_0'=4,'dp_1'=4,'dp_2'=4,'rep'=2] {'dp_1'}, use_global_device_ids=true, to_apply=%region_3.0 | all-reduce | flops 1 | bytes 8 | tf_op jit(solution)/shard_map/psum | solution.py:45
  161.8 11.0 %psum.30 = f32[]{:T(128)} all-reduce(f32[]{:T(128)} %psum.29), channel_id=1, replica_groups=mesh['dp_0'=4,'dp_1'=4,'dp_2'=4,'rep'=2] {'dp_2'}, use_global_device_ids=true, to_apply=%region_4.0 | all-reduce | flops 1 | bytes 8 | tf_op jit(solution)/shard_map/psum | solution.py:45
  172.9 3.1 %psum.31 = f32[]{:T(128)} all-reduce(f32[]{:T(128)} %psum.30), channel_id=1, replica_groups=mesh['dp_0'=4,'dp_1'=4,'dp_2'=4,'rep'=2] {'rep'}, use_global_device_ids=true, to_apply=%region_5.6 | all-reduce | flops 1 | bytes 8 | tf_op jit(solution)/shard_map/psum | solution.py:45
  176.7 64.0 %all-reduce.1 = f32[2,3456]{1,0:T(2,128)S(1)} all-reduce(f32[2,3456]{1,0:T(2,128)S(1)} %pad_maximum_fusion.2), channel_id=3, replica_groups=mesh['dp_0'=4,'dp_1'=4,'dp_2'=4,'rep'=2] {'dp_0','dp_1','dp_2','rep'}, use_global_device_ids=true, to_apply=%region_9.10.clone | all-reduce | flops 6912 | bytes 55296
  240.7 0.6 dynamic-slice_multiply_fusion
  241.5 4.6 %all_to_all.32 = bf16[16,1,2,1,64,1,256]{6,0,4,5,3,1,2:T(8,128)(2,1)S(1)} all-to-all(bf16[16,1,2,1,64,1,256]{6,0,4,5,3,1,2:T(8,128)(2,1)S(1)} %copy.81), channel_id=1, replica_groups=mesh['dp_0'=4,'dp_1'=4,'dp_2'=4,'rep'=2] {'rep'}, dimensions={2} | all-to-all | bytes 2097152 | tf_op jit(solution)/shard_map/all_to_all | solution.py:203
  246.3 1.6 copy.82
  248.0 4.1 %mul.105 = f32[16,1,32768]{2,1,0:T(1,128)} reshape(f32[16,1,1,1,64,2,1,256]{7,5,4,0,6,3,2,1:T(2,128)S(1)} %copy.82) | data formatting | bytes 4194304 | tf_op jit(solution)/shard_map/mul | solution.py:220
  252.1 33.3 %reduce-scatter.5.cloned.1.call-done = bf16[216,128]{1,0:T(8,128)(2,1)} async-done(((bf16[27648,128]{1,0:T(8,128)(2,1)}), bf16[216,128]{1,0:T(8,128)(2,1)}) %reduce-scatter.5.cloned.1.call-update) | async-done | bytes 55312
  285.4 0.8 convert_element_type.92
  286.2 0.7 copy.85
  286.9 0.7 copy.86
  (88 shorter events, 6.3 us)
Async XLA Ops:
  7.2 36.8 %copy-start = (bf16[6,256,128]{2,1,0:T(8,128)(2,1)S(1)}, bf16[6,256,128]{2,1,0:T(8,128)(2,1)}, u32[]{:S(2)}) copy-start(bf16[6,256,128]{2,1,0:T(8,128)(2,1)} %param.17) | copy-start | bytes 1179652
  8.9 13.0 %copy-start.10 = (bf16[128,256]{1,0:T(8,128)(2,1)S(1)}, bf16[128,256]{1,0:T(8,128)(2,1)}, u32[]{:S(2)}) copy-start(bf16[128,256]{1,0:T(8,128)(2,1)} %param.14) | copy-start | bytes 196612
  8.9 13.7 %copy-start.13 = (f32[3456]{0:T(1024)S(1)}, f32[3456]{0:T(1024)}, u32[]{:S(2)}) copy-start(f32[3456]{0:T(1024)} %param.23) | copy-start | bytes 41476
  8.9 14.3 %copy-start.26 = (s32[128]{0:T(128)S(1)}, s32[128]{0:T(128)}, u32[]{:S(2)}) copy-start(s32[128]{0:T(128)} %param.13) | copy-start | bytes 1540
  8.9 14.3 %copy-start.15 = (f32[2,3456]{1,0:T(2,128)S(1)}, f32[2,3456]{1,0:T(2,128)}, u32[]{:S(2)}) copy-start(f32[2,3456]{1,0:T(2,128)} %param.22) | copy-start | bytes 82948
  10.6 30.3 %all-to-all-start = ((bf16[128,16,1,1,1,256]{5,1,4,3,2,0:T(8,128)(2,1)}), bf16[128,16,1,1,1,256]{5,1,4,3,2,0:T(8,128)(2,1)S(1)}, u32[]{:S(2)}, u32[]{:S(2)}) async-start(bf16[128,16,1,1,1,256]{5,1,4,3,2,0:T(8,128)(2,1)} %bitcast.2), calls=%async_computation | async-start | bytes 2097152 | tf_op jit(solution)/shard_map/all_to_all | solution.py:38
  21.8 20.1 %copy-start.9 = (bf16[16,16,128]{2,1,0:T(8,128)(2,1)S(1)}, bf16[16,16,128]{2,1,0:T(8,128)(2,1)}, u32[]{:S(2)}) copy-start(bf16[16,16,128]{2,1,0:T(8,128)(2,1)} %param.19) | copy-start | bytes 196612
  21.8 263.6 %reduce-scatter.5.cloned.1.call-start = ((), (), s32[]{:S(2)}) async-start(), calls=%async_computation.4 | async-start | bytes 7133184
  23.2 19.2 %copy-start.22 = (s32[128]{0:T(128)}, s32[128]{0:T(128)S(1)}, u32[]{:S(2)}) copy-start(s32[128]{0:T(128)S(1)} %compare_select_fusion) | copy-start | bytes 1540
  41.8 1.4 copy-start.7
  43.5 0.9 copy-start.11
  43.7 15.5 %copy-start.8 = (bf16[512,256]{0,1:T(8,128)(2,1)}, bf16[512,256]{0,1:T(8,128)(2,1)S(1)}, u32[]{:S(2)}) copy-start(bf16[512,256]{0,1:T(8,128)(2,1)S(1)} %copy.75) | copy-start | bytes 786436
  44.5 14.8 %copy-start.6 = (bf16[768,256]{0,1:T(8,128)(2,1)}, bf16[768,256]{0,1:T(8,128)(2,1)S(1)}, u32[]{:S(2)}) copy-start(bf16[768,256]{0,1:T(8,128)(2,1)S(1)} %copy.74) | copy-start | bytes 1179652
  44.5 2.7 copy-start.4
  44.5 2.7 copy-start.18
  47.2 2.7 copy-start.5
  50.5 0.8 copy-start.12
  50.6 0.8 copy-start.19
  51.4 1.8 copy-start.1
  51.4 1.8 copy-start.24
  51.4 1.8 copy-start.25
  51.4 2.4 copy-start.14
  53.8 2.8 copy-start.20
  58.4 1.8 copy-start.3
  75.1 3.9 %copy-start.2 = (bf16[1,128,27,256]{3,2,1,0:T(8,128)(2,1)S(1)}, bf16[1,128,27,256]{3,2,1,0:T(8,128)(2,1)}, u32[]{:S(2)}) copy-start(bf16[1,128,27,256]{3,2,1,0:T(8,128)(2,1)} %concatenate.29) | copy-start | bytes 5308420
  106.3 0.7 copy-start.21
  114.5 1.8 copy-start.23
  128.1 47.8 %copy-start.17 = (f32[3456]{0:T(1024)S(1)}, f32[3456]{0:T(1024)}, u32[]{:S(2)}) copy-start(f32[3456]{0:T(1024)} %get-tuple-element.21) | copy-start | bytes 41476
  128.1 47.8 %copy-start.16 = (f32[3456]{0:T(1024)S(1)}, f32[3456]{0:T(1024)}, u32[]{:S(2)}) copy-start(f32[3456]{0:T(1024)} %get-tuple-element.20) | copy-start | bytes 41476
  129.2 112.2 %all-to-all-start.1 = ((bf16[16,64,2,1,1,1,256]{6,0,2,5,4,3,1:T(8,128)(2,1)}), bf16[16,64,2,1,1,1,256]{6,0,2,5,4,3,1:T(8,128)(2,1)S(1)}, u32[]{:S(2)}, u32[]{:S(2)}) async-start(bf16[16,64,2,1,1,1,256]{6,0,2,5,4,3,1:T(8,128)(2,1)} %bitcast.47), calls=%async_computation.1 | async-start | bytes 2097152 | tf_op jit(solution)/shard_map/all_to_all | solution.py:204
Sparse Core Ops, SparseCore 0:
  106.4 178.8 reduce-scatter.4
where the time goes:
time: 296 us; the launch traced here: 294 us
  blocking collectives  110 us (37%)
  local copies, waits for them, and re-layouts  63.9 us (22%)
  waiting for transfers between devices  50.3 us (17%)
  matrix products  26.4 us (9%)
  starting transfers between devices  16.1 us (5%)
  between operations  15.3 us (5%)
  other arithmetic  12 us (4%)
    unnamed x1, blocking collectives  64 us
    psum x4, blocking collectives, one_axis_at_a_time(): shard = lax.psum(shard, axis)  41.8 us
    unnamed x2, waiting for transfers between devices  33.3 us
    all_to_all x1, waiting for transfers between devices, one_exchange(): tiles = lax.all_to_all(tiles, axis, split_axis=0, concat_axis=0, tiled=True)  17 us
    concatenate x4, local copies, waits for them, and re-layouts, body(): weight_terms = jnp.concatenate([in_term, out_term], 0)  13.1 us
    reshape x1, local copies, waits for them, and re-layouts, own_tiles(): jnp.pad(lines, ((0, 0), (0, extent * 128 - lines.shape[1])))  12.5 us
    scatter x1, local copies, waits for them, and re-layouts, block_step(): jnp.zeros(logical_grad.shape, jnp.float32).at[:, slot_of_block, :]  11.9 us
    all_to_all x1, starting transfers between devices, one_exchange(): tiles = lax.all_to_all(tiles, axis, split_axis=0, concat_axis=0, tiled=True)  11.2 us
  transfers between devices with their start and end apart: 3, of which 2 were waited for; matrix products, arithmetic and copies ran while one was open for 11% of the time, Pallas kernels for 0%

commit v1 on v0

--- a/solution.py
+++ b/solution.py
@@ -42,7 +42,7 @@
 
 def one_axis_at_a_time(shard, axes):
     for axis in axes:
-        shard = lax.psum(shard, axis)
+        shard = jnp.sum(lax.all_gather(shard, axis), axis=0)
     return shard
 
 

time: 296 us -> 296 us (level)
  local copies, waits for them, and re-layouts: 63.9 us -> 72.1 us
  blocking collectives: 110 us -> 104 us
  waiting for transfers between devices: 50.3 us -> 45.5 us
    psum x4 -> x0, blocking collectives: 41.8 us -> none  [one_axis_at_a_time(): shard = lax.psum(shard, axis)]
    unnamed x1 -> x5, blocking collectives: 64 us -> 99.5 us
    unnamed x59 -> x79, local copies, waits for them, and re-layouts: 6.85 us -> 15.1 us
    unnamed x2, waiting for transfers between devices: 33.3 us -> 28.4 us
  transfers between devices with their start and end apart: 3 -> 3, of which waited for: 2 -> 2; matrix products, arithmetic and copies ran while one was open for 11% -> 14% of each run, Pallas kernels for 0% -> 0%
where the time goes in v1:
time: 296 us; the launch traced here: 294 us
  blocking collectives  104 us (35%)
  local copies, waits for them, and re-layouts  72.1 us (24%)
  waiting for transfers between devices  45.5 us (15%)
  matrix products  26.4 us (9%)
  starting transfers between devices  16.1 us (5%)
  between operations  15.3 us (5%)
  other arithmetic  14.5 us (5%)
    unnamed x5, blocking collectives  99.5 us
    unnamed x2, waiting for transfers between devices  28.4 us
    all_to_all x1, waiting for transfers between devices, one_exchange(): tiles = lax.all_to_all(tiles, axis, split_axis=0, concat_axis=0, tiled=True)  17 us
    unnamed x79, local copies, waits for them, and re-layouts  15.1 us
    concatenate x4, local copies, waits for them, and re-layouts, body(): weight_terms = jnp.concatenate([in_term, out_term], 0)  13.1 us
    reshape x1, local copies, waits for them, and re-layouts, own_tiles(): jnp.pad(lines, ((0, 0), (0, extent * 128 - lines.shape[1])))  12.5 us
    scatter x1, local copies, waits for them, and re-layouts, block_step(): jnp.zeros(logical_grad.shape, jnp.float32).at[:, slot_of_block, :]  11.9 us
    all_to_all x1, starting transfers between devices, one_exchange(): tiles = lax.all_to_all(tiles, axis, split_axis=0, concat_axis=0, tiled=True)  11.2 us
  transfers between devices with their start and end apart: 3, of which 2 were waited for; matrix products, arithmetic and copies ran while one was open for 14% of the time, Pallas kernels for 0%

profile of v1, /device:TPU:0, one launch (start us, length us, event | category | flops | bytes accessed | tf_op | source)
XLA Modules:
  0.0 294.0 jit_solution(14252410114949591150)
XLA Ops:
  7.2 1.6 copy.94
  9.1 1.6 copy.69
  10.6 11.2 %all-to-all-start = ((bf16[128,16,1,1,1,256]{5,1,4,3,2,0:T(8,128)(2,1)}), bf16[128,16,1,1,1,256]{5,1,4,3,2,0:T(8,128)(2,1)S(1)}, u32[]{:S(2)}, u32[]{:S(2)}) async-start(bf16[128,16,1,1,1,256]{5,1,4,3,2,0:T(8,128)(2,1)} %bitcast.2), calls=%async_computation | async-start | bytes 2097152 | tf_op jit(solution)/shard_map/all_to_all | solution.py:38
  21.9 0.7 copy.73
  23.2 0.7 slice_reduce_fusion
  23.9 17.0 %all-to-all-done = bf16[128,16,1,1,1,256]{5,1,4,3,2,0:T(8,128)(2,1)S(1)} async-done(((bf16[128,16,1,1,1,256]{5,1,4,3,2,0:T(8,128)(2,1)}), bf16[128,16,1,1,1,256]{5,1,4,3,2,0:T(8,128)(2,1)S(1)}, u32[]{:S(2)}, u32[]{:S(2)}) %all-to-all-start) | async-done | bytes 1048608 | tf_op jit(solution)/shard_map/all_to_all | solution.py:38
  42.4 0.8 copy.76
  44.5 2.3 fusion.37
  47.2 2.5 fusion.8
  51.4 1.7 fusion.13
  53.2 0.7 fusion.56
  53.9 0.7 fusion.46
  54.6 2.0 convolution_convert_fusion
  56.7 1.8 fusion.11
  58.4 0.8 fusion.40
  59.3 0.9 copy-done.3
  60.3 2.0 convolution_convert_fusion.1
  62.3 0.7 convolution_convert_fusion.2
  63.0 3.8 %concatenate.29 = bf16[1,128,27,256]{3,2,1,0:T(8,128)(2,1)} reshape(bf16[3456,256]{1,0:T(8,128)(2,1)} %convolution_convert_fusion) | data formatting | bytes 3538944 | tf_op jit(solution)/shard_map/concatenate | solution.py:213
  66.8 3.8 %concatenate.28 = bf16[1,128,27,256]{3,2,1,0:T(8,128)(2,1)} reshape(bf16[3456,256]{1,0:T(8,128)(2,1)} %convolution_convert_fusion.1) | data formatting | bytes 3538944 | tf_op jit(solution)/shard_map/concatenate | solution.py:213
  70.6 1.6 concatenate.27
  72.2 3.0 %convolution_convert_fusion.3 = bf16[3456,256]{1,0:T(8,128)(2,1)} fusion(bf16[256,256]{1,0:T(8,128)(2,1)S(1)} %fusion.40, bf16[2048,256]{0,1:T(8,128)(2,1)S(1)} %copy.76, bf16[512,256]{0,1:T(8,128)(2,1)} %copy-done.8, bf16[768,256]{0,1:T(8,128)(2,1)} %copy-done.6, bf16[128,256]{0,1:T(8,128)(2,1)S(1)} %copy-done.12), kind=kOutput, calls=%fused_computation.22 | convolution fusion | flops 460947456 | bytes 3670016 | tf_op jit(solution)/shard_map/wr,kr->wk/dot_general | solution.py:148
  75.2 3.9 %concatenate.26 = bf16[1,128,27,256]{3,2,1,0:T(8,128)(2,1)} reshape(bf16[3456,256]{1,0:T(8,128)(2,1)} %convolution_convert_fusion.3) | data formatting | bytes 3538944 | tf_op jit(solution)/shard_map/concatenate | solution.py:213
  79.1 6.7 %maximum_bitcast_fusion = bf16[128,4,27,256]{3,2,0,1:T(8,128)(2,1)} fusion(bf16[1,128,27,256]{3,2,1,0:T(8,128)(2,1)S(1)} %copy-done.2, bf16[1,128,27,256]{3,2,1,0:T(8,128)(2,1)} %concatenate.28, bf16[1,128,27,256]{3,2,1,0:T(8,128)(2,1)} %concatenate.27, bf16[1,128,27,256]{3,2,1,0:T(8,128)(2,1)} %concatenate.26), kind=kLoop, calls=%fused_computation.2 | loop fusion | flops 10616832 | bytes 14155776 | tf_op jit(solution)/shard_map/transpose | solution.py:23
  85.8 8.0 %copy.83 = bf16[128,4,27,256]{3,2,1,0:T(8,128)(2,1)} copy(bf16[128,4,27,256]{3,2,0,1:T(8,128)(2,1)} %maximum_bitcast_fusion) | data formatting | bytes 14155776 | tf_op jit(solution)/shard_map/transpose | solution.py:23
  93.8 12.5 %reshape.162 = bf16[27648,128]{1,0:T(8,128)(2,1)} reshape(bf16[128,4,27,256]{3,2,1,0:T(8,128)(2,1)} %copy.83) | data formatting | bytes 14155776 | tf_op jit(solution)/shard_map/reshape | solution.py:54
  107.0 5.7 %fusion.4 = bf16[3456,256]{0,1:T(8,128)(2,1)S(1)} fusion(f32[3456,256]{0,1:T(8,128)} %copy-done.3, bf16[256,256]{1,0:T(8,128)(2,1)S(1)} %fusion.40, f32[3456,256]{0,1:T(8,128)} %copy-done.1, f32[3456,256]{0,1:T(8,128)} %get-tuple-element.31, f32[256]{0:T(256)S(1)} %copy-done.21, f32[3456]{0:T(1024)S(1)} %copy-done.14, bf16[2,3456,256]{2,1,0:T(8,128)(2,1)} %param.20), kind=kOutput, calls=%fused_computation.18 | convolution fusion | flops 459177984 | bytes 14301696 | tf_op jit(solution)/shard_map/wk,kr->wr/dot_general | solution.py:152
  114.5 1.5 maximum_bitcast_fusion.1
  116.3 11.9 %scatter_fusion = f32[16,128,256]{2,0,1:T(8,128)S(1)} fusion(f32[16,128,256]{2,0,1:T(8,128)S(1)} %broadcast_in_dim.18, s32[128]{0:T(128)S(1)} %copy-done.23, f32[128,16,256]{2,1,0:T(8,128)} %maximum_bitcast_fusion.1), kind=kCustom, calls=%fused_computation.1 | custom fusion | bytes 6291968 | tf_op jit(solution)/shard_map/scatter | solution.py:158
  128.2 1.1 convert_element_type.89
  129.3 4.9 %all-to-all-start.1 = ((bf16[16,64,2,1,1,1,256]{6,0,2,5,4,3,1:T(8,128)(2,1)}), bf16[16,64,2,1,1,1,256]{6,0,2,5,4,3,1:T(8,128)(2,1)S(1)}, u32[]{:S(2)}, u32[]{:S(2)}) async-start(bf16[16,64,2,1,1,1,256]{6,0,2,5,4,3,1:T(8,128)(2,1)} %bitcast.47), calls=%async_computation.1 | async-start | bytes 2097152 | tf_op jit(solution)/shard_map/all_to_all | solution.py:204
  134.9 0.7 dynamic-slice.1
  136.2 1.4 dynamic-update-slice
  138.2 12.1 %all-reduce = f32[4]{0:T(128)S(1)} all-reduce(f32[4]{0:T(128)S(1)} %dynamic-update-slice), channel_id=1, replica_groups=mesh['dp_0'=4,'dp_1'=4,'dp_2'=4,'rep'=2] {'dp_0'}, use_global_device_ids=true, to_apply=%add | all-reduce | flops 4 | bytes 32
  151.0 1.4 dynamic-update-slice.1
  152.4 10.5 %all-reduce.1 = f32[4]{0:T(128)S(1)} all-reduce(f32[4]{0:T(128)S(1)} %dynamic-update-slice.1), channel_id=1, replica_groups=mesh['dp_0'=4,'dp_1'=4,'dp_2'=4,'rep'=2] {'dp_1'}, use_global_device_ids=true, to_apply=%add.1 | all-reduce | flops 4 | bytes 32
  163.5 1.4 dynamic-update-slice.2
  164.9 10.4 %all-reduce.2 = f32[4]{0:T(128)S(1)} all-reduce(f32[4]{0:T(128)S(1)} %dynamic-update-slice.2), channel_id=1, replica_groups=mesh['dp_0'=4,'dp_1'=4,'dp_2'=4,'rep'=2] {'dp_2'}, use_global_device_ids=true, to_apply=%add.2 | all-reduce | flops 4 | bytes 32
  175.9 1.4 dynamic-update-slice.3
  177.3 2.4 all-reduce.3
  181.1 64.1 %all-reduce.5 = f32[2,3456]{1,0:T(2,128)S(1)} all-reduce(f32[2,3456]{1,0:T(2,128)S(1)} %pad_maximum_fusion.2), channel_id=3, replica_groups=mesh['dp_0'=4,'dp_1'=4,'dp_2'=4,'rep'=2] {'dp_0','dp_1','dp_2','rep'}, use_global_device_ids=true, to_apply=%region_9.10.clone | all-reduce | flops 6912 | bytes 55296
  245.9 4.6 %all_to_all.32 = bf16[16,1,2,1,64,1,256]{6,0,4,5,3,1,2:T(8,128)(2,1)S(1)} all-to-all(bf16[16,1,2,1,64,1,256]{6,0,4,5,3,1,2:T(8,128)(2,1)S(1)} %copy.81), channel_id=1, replica_groups=mesh['dp_0'=4,'dp_1'=4,'dp_2'=4,'rep'=2] {'rep'}, dimensions={2} | all-to-all | bytes 2097152 | tf_op jit(solution)/shard_map/all_to_all | solution.py:203
  250.8 1.6 copy.82
  252.4 4.1 %mul.105 = f32[16,1,32768]{2,1,0:T(1,128)} reshape(f32[16,1,1,1,64,2,1,256]{7,5,4,0,6,3,2,1:T(2,128)S(1)} %copy.82) | data formatting | bytes 4194304 | tf_op jit(solution)/shard_map/mul | solution.py:220
  256.5 28.4 %reduce-scatter.5.cloned.1.call-done = bf16[216,128]{1,0:T(8,128)(2,1)} async-done(((bf16[27648,128]{1,0:T(8,128)(2,1)}), bf16[216,128]{1,0:T(8,128)(2,1)}) %reduce-scatter.5.cloned.1.call-update) | async-done | bytes 55312
  284.9 0.8 convert_element_type.92
  285.8 0.7 copy.85
  286.5 0.7 copy.86
  (112 shorter events, 13.8 us)
Async XLA Ops:
  7.2 36.8 %copy-start = (bf16[6,256,128]{2,1,0:T(8,128)(2,1)S(1)}, bf16[6,256,128]{2,1,0:T(8,128)(2,1)}, u32[]{:S(2)}) copy-start(bf16[6,256,128]{2,1,0:T(8,128)(2,1)} %param.17) | copy-start | bytes 1179652
  8.9 13.0 %copy-start.10 = (bf16[128,256]{1,0:T(8,128)(2,1)S(1)}, bf16[128,256]{1,0:T(8,128)(2,1)}, u32[]{:S(2)}) copy-start(bf16[128,256]{1,0:T(8,128)(2,1)} %param.14) | copy-start | bytes 196612
  8.9 13.7 %copy-start.13 = (f32[3456]{0:T(1024)S(1)}, f32[3456]{0:T(1024)}, u32[]{:S(2)}) copy-start(f32[3456]{0:T(1024)} %param.23) | copy-start | bytes 41476
  8.9 14.3 %copy-start.26 = (s32[128]{0:T(128)S(1)}, s32[128]{0:T(128)}, u32[]{:S(2)}) copy-start(s32[128]{0:T(128)} %param.13) | copy-start | bytes 1540
  8.9 14.3 %copy-start.15 = (f32[2,3456]{1,0:T(2,128)S(1)}, f32[2,3456]{1,0:T(2,128)}, u32[]{:S(2)}) copy-start(f32[2,3456]{1,0:T(2,128)} %param.22) | copy-start | bytes 82948
  10.6 30.3 %all-to-all-start = ((bf16[128,16,1,1,1,256]{5,1,4,3,2,0:T(8,128)(2,1)}), bf16[128,16,1,1,1,256]{5,1,4,3,2,0:T(8,128)(2,1)S(1)}, u32[]{:S(2)}, u32[]{:S(2)}) async-start(bf16[128,16,1,1,1,256]{5,1,4,3,2,0:T(8,128)(2,1)} %bitcast.2), calls=%async_computation | async-start | bytes 2097152 | tf_op jit(solution)/shard_map/all_to_all | solution.py:38
  21.8 20.1 %copy-start.9 = (bf16[16,16,128]{2,1,0:T(8,128)(2,1)S(1)}, bf16[16,16,128]{2,1,0:T(8,128)(2,1)}, u32[]{:S(2)}) copy-start(bf16[16,16,128]{2,1,0:T(8,128)(2,1)} %param.19) | copy-start | bytes 196612
  21.8 263.1 %reduce-scatter.5.cloned.1.call-start = ((), (), s32[]{:S(2)}) async-start(), calls=%async_computation.4 | async-start | bytes 7133184
  23.2 19.2 %copy-start.22 = (s32[128]{0:T(128)}, s32[128]{0:T(128)S(1)}, u32[]{:S(2)}) copy-start(s32[128]{0:T(128)S(1)} %compare_select_fusion) | copy-start | bytes 1540
  41.8 1.4 copy-start.7
  43.5 0.9 copy-start.11
  43.7 15.6 %copy-start.8 = (bf16[512,256]{0,1:T(8,128)(2,1)}, bf16[512,256]{0,1:T(8,128)(2,1)S(1)}, u32[]{:S(2)}) copy-start(bf16[512,256]{0,1:T(8,128)(2,1)S(1)} %copy.75) | copy-start | bytes 786436
  44.5 14.8 %copy-start.6 = (bf16[768,256]{0,1:T(8,128)(2,1)}, bf16[768,256]{0,1:T(8,128)(2,1)S(1)}, u32[]{:S(2)}) copy-start(bf16[768,256]{0,1:T(8,128)(2,1)S(1)} %copy.74) | copy-start | bytes 1179652
  44.5 2.7 copy-start.4
  44.5 2.7 copy-start.18
  47.2 2.7 copy-start.5
  50.5 0.8 copy-start.12
  50.6 0.8 copy-start.19
  51.4 1.8 copy-start.1
  51.4 1.8 copy-start.24
  51.4 1.8 copy-start.25
  51.4 2.5 copy-start.14
  53.9 2.8 copy-start.20
  58.4 1.8 copy-start.3
  75.2 3.9 %copy-start.2 = (bf16[1,128,27,256]{3,2,1,0:T(8,128)(2,1)S(1)}, bf16[1,128,27,256]{3,2,1,0:T(8,128)(2,1)}, u32[]{:S(2)}) copy-start(bf16[1,128,27,256]{3,2,1,0:T(8,128)(2,1)} %concatenate.29) | copy-start | bytes 5308420
  106.4 0.7 copy-start.21
  114.5 1.8 copy-start.23
  128.2 6.1 %copy-start.30 = (u32[128]{0:T(128)S(1)}, u32[128]{0:T(128)}, u32[]{:S(2)}) copy-start(u32[128]{0:T(128)} %constant.29) | copy-start | bytes 1540
  128.2 6.7 %copy-start.29 = (u32[128]{0:T(128)S(1)}, u32[128]{0:T(128)}, u32[]{:S(2)}) copy-start(u32[128]{0:T(128)} %constant.34) | copy-start | bytes 1540
  128.2 7.3 %copy-start.28 = (u32[128]{0:T(128)S(1)}, u32[128]{0:T(128)}, u32[]{:S(2)}) copy-start(u32[128]{0:T(128)} %constant.39) | copy-start | bytes 1540
  128.2 9.4 %copy-start.27 = (u32[128]{0:T(128)S(1)}, u32[128]{0:T(128)}, u32[]{:S(2)}) copy-start(u32[128]{0:T(128)} %constant.44) | copy-start | bytes 1540
  128.2 51.5 %copy-start.17 = (f32[3456]{0:T(1024)S(1)}, f32[3456]{0:T(1024)}, u32[]{:S(2)}) copy-start(f32[3456]{0:T(1024)} %get-tuple-element.21) | copy-start | bytes 41476
  128.2 51.5 %copy-start.16 = (f32[3456]{0:T(1024)S(1)}, f32[3456]{0:T(1024)}, u32[]{:S(2)}) copy-start(f32[3456]{0:T(1024)} %get-tuple-element.20) | copy-start | bytes 41476
  129.3 116.5 %all-to-all-start.1 = ((bf16[16,64,2,1,1,1,256]{6,0,2,5,4,3,1:T(8,128)(2,1)}), bf16[16,64,2,1,1,1,256]{6,0,2,5,4,3,1:T(8,128)(2,1)S(1)}, u32[]{:S(2)}, u32[]{:S(2)}) async-start(bf16[16,64,2,1,1,1,256]{6,0,2,5,4,3,1:T(8,128)(2,1)} %bitcast.47), calls=%async_computation.1 | async-start | bytes 2097152 | tf_op jit(solution)/shard_map/all_to_all | solution.py:204
Sparse Core Ops, SparseCore 0:
  106.5 178.3 reduce-scatter.4
